TPU v7x, 512 devices: a whole 4x4x16 slice. The times are simulated.
512 devices in a mesh: ctx: 16 (over y, z_lo), exp: 32 (over z_hi, x, core).
Axes of the slice: x: 4, y: 4, z: 16 (z_hi: 4, z_lo: 4; z = z_hi * 4 + z_lo), core: 2. Of those that a mesh axis runs over, the one named last changes fastest.
Arguments:
- query: bfloat16 [32, 1024, 2048], P('exp', 'ctx'), may hold values from -24 to 24
- key_value: bfloat16 [32, 1024, 2, 256], P('exp', 'ctx'), may hold values from -24 to 24
- positions: int32 [32, 1024], P('exp', 'ctx'), may hold values from 0 to 1023, as said below
- resid: bfloat16 [32, 1024, 1440], P('exp', 'ctx'), may hold values from -6 to 6
- sinks: float32 [32], replicated, may hold values from -2 to 3
- o_weight: bfloat16 [2048, 1440], P('exp'), may hold values from -0.125 to 0.125
- norm_gain: float32 [1440], replicated, may hold values from 0.25 to 1.75
- expert_ids: int32 [32, 1024, 4], P('exp', 'ctx'), may hold values from 0 to 127, all different within a row; in each aligned block of 64 rows (0 to 63, 64 to 127, ..., all dimensions but the last counted through in order) at most 2 rows name the same one
- route_weights: float32 [32, 1024, 4], P('exp', 'ctx'), may hold values from 0.1 to 0.5
- w_gate: bfloat16 [1440, 184320], P(None, ('ctx', 'exp')), may hold values from -0.15625 to 0.15625
- w_up: bfloat16 [1440, 184320], P(None, ('ctx', 'exp')), may hold values from -0.15625 to 0.15625
- w_down: bfloat16 [184320, 1440], P(('ctx', 'exp')), may hold values from -0.15625 to 0.15625
Outputs:
- out: bfloat16 [32, 1024, 1440], P('exp', 'ctx')
Inputs may be any that keep to these rules, and one draw needn't show every extreme that they name: Within each sequence every position appears once; the 64 stored rows of one device are two runs of 32 consecutive ascending positions, each run starting at a multiple of 32. `expert_ids`: each row names 4 different experts; among the 64 rows of one device no expert is named more than 2 times, a bound that some block reaches.
All inputs are finite; a program needn't handle non-finite values.
Results may differ from a plain program's by a relative error of at most 0.0075.
Values may be sent and summed in bfloat16 or wider, within the bound.
No kernel may reach another device: no remote copies, remote signals or barrier semaphores. Data moves between devices by JAX's collectives and lax.ppermute only.
A program may use at most 64 MiB of HBM per device.

v0:
```python
import math

import jax
import jax.numpy as jnp
from jax import lax
from jax.sharding import PartitionSpec as P

D = 1440
QH = 32
KVH = 4
HD = 64
TOP = 4
SLICES = 4


NEG_FILL = -1e30


def passed_along(value, axis, by):
    length = lax.axis_size(axis)
    return lax.ppermute(value, axis, [(i, (i + by) % length) for i in range(length)])


def attend_block(grouped, keys, values, query_pos, key_pos, state):
    run_max, run_sum, accum = state
    scores = jnp.einsum("rgjd,sgd->gjrs", grouped, keys, preferred_element_type=jnp.float32) * (
        1.0 / math.sqrt(HD)
    )
    allowed = key_pos[None, :] <= query_pos[:, None]
    scores = jnp.where(allowed[None, None], scores, NEG_FILL)
    new_max = jnp.maximum(run_max, jnp.max(scores, axis=-1))
    factor = jnp.exp(run_max - new_max)
    weights = jnp.exp(scores - new_max[..., None])
    run_sum = run_sum * factor + jnp.sum(weights, axis=-1)
    accum = accum * factor[..., None] + jnp.einsum(
        "gjrs,sgd->gjrd", weights, values.astype(jnp.float32), precision=lax.Precision.HIGHEST
    )
    return (new_max, run_sum, accum)


def body(
    query,
    key_value,
    positions,
    resid,
    sinks,
    o_weight,
    norm_gain,
    expert_ids,
    route_weights,
    w_gate,
    w_up,
    w_down,
):
    rows = query.shape[1]
    group = QH // KVH
    grouped = query[0].reshape(rows, KVH, group, HD)
    own_kv = key_value[0]
    own_pos = positions[0]
    start_max = jnp.broadcast_to(sinks.reshape(KVH, group)[:, :, None], (KVH, group, rows))
    state = (
        start_max,
        jnp.ones((KVH, group, rows), jnp.float32),
        jnp.zeros((KVH, group, rows, HD), jnp.float32),
    )

    def take(block, block_pos, carry):
        width = block.shape[0]
        keys = block[:, 0].reshape(width, KVH, HD)
        values = block[:, 1].reshape(width, KVH, HD)
        return attend_block(grouped, keys, values, own_pos, block_pos, carry)

    state = take(own_kv, own_pos, state)

    def turn(step, carry):
        block, block_pos, inner = carry
        block, block_pos = passed_along((block, block_pos), "ctx", 1)
        return (block, block_pos, take(block, block_pos, inner))

    state = lax.fori_loop(0, lax.axis_size("ctx") - 1, turn, (own_kv, own_pos, state))[2]
    run_max, run_sum, accum = state
    attended = accum / run_sum[..., None]
    attended = jnp.transpose(attended, (2, 0, 1, 3)).reshape(rows, QH * HD).astype(jnp.bfloat16)
    projected = jnp.dot(
        attended,
        lax.all_gather(o_weight, "exp", axis=0, tiled=True),
        preferred_element_type=jnp.float32,
    )
    mixed = resid[0].astype(jnp.float32) + projected
    normed = (
        mixed * lax.rsqrt(jnp.mean(mixed * mixed, axis=-1, keepdims=True) + 1e-05) * norm_gain
    ).astype(jnp.bfloat16)
    n_ctx = lax.axis_size("ctx")
    n_exp = lax.axis_size("exp")
    n_experts = n_ctx * n_exp // SLICES
    per_row = n_exp // SLICES
    cap = max(2, rows * TOP // n_experts)
    n_slots = n_experts * cap
    chosen = expert_ids[0].reshape(rows * TOP)
    onehot = (chosen[:, None] == jnp.arange(n_experts, dtype=jnp.int32)[None, :]).astype(jnp.int32)
    rank = jnp.sum((jnp.cumsum(onehot, axis=0) - onehot) * onehot, axis=1)
    slot = (chosen % per_row * n_ctx + chosen // per_row) * cap + rank
    source = (
        jnp.zeros((n_slots,), jnp.int32)
        .at[slot]
        .set(jnp.arange(rows * TOP, dtype=jnp.int32) // TOP)
    )
    filled = jnp.zeros((n_slots,), jnp.bool_).at[slot].set(True)
    outgoing = jnp.where(filled[:, None], normed[source], jnp.zeros((), jnp.bfloat16)).reshape(
        per_row, n_ctx, cap, D
    )
    arrived = lax.all_to_all(outgoing, "ctx", split_axis=1, concat_axis=1, tiled=True)
    copies = jnp.repeat(arrived, SLICES, axis=0)
    block = lax.all_to_all(copies, "exp", split_axis=0, concat_axis=0, tiled=True)
    flat = block.reshape(-1, D)
    gate = jnp.dot(flat, w_gate, preferred_element_type=jnp.float32)
    lifted = jnp.dot(flat, w_up, preferred_element_type=jnp.float32)
    active = (gate * jax.nn.sigmoid(1.702 * gate) * (lifted + 1.0)).astype(jnp.bfloat16)
    back = lax.all_to_all(
        jnp.dot(active, w_down, preferred_element_type=jnp.float32)
        .astype(jnp.bfloat16)
        .reshape(block.shape),
        "exp",
        split_axis=0,
        concat_axis=0,
        tiled=True,
    )
    count = back.shape[1]
    summed = jnp.sum(back.reshape(per_row, SLICES, count, cap, D).astype(jnp.float32), axis=1)
    result = summed.astype(jnp.bfloat16)
    returned = lax.all_to_all(result, "ctx", split_axis=1, concat_axis=1, tiled=True)
    picked = returned.reshape(n_slots, D)[slot].astype(jnp.float32).reshape(rows, TOP, D)
    final = mixed + jnp.sum(route_weights[0][:, :, None] * picked, axis=1)
    return final.astype(jnp.bfloat16)[None]


def solution(mesh):
    return jax.shard_map(
        body,
        mesh=mesh,
        in_specs=(
            P("exp", "ctx", None),
            P("exp", "ctx", None, None),
            P("exp", "ctx"),
            P("exp", "ctx", None),
            P(),
            P("exp", None),
            P(),
            P("exp", "ctx", None),
            P("exp", "ctx", None),
            P(None, ("ctx", "exp")),
            P(None, ("ctx", "exp")),
            P(("ctx", "exp"), None),
        ),
        out_specs=P("exp", "ctx", None),
        check_vma=False,
    )
```

profile of v0, /device:TPU:1, one launch (start us, length us, event | category | flops | bytes accessed | tf_op | source)
XLA Modules:
  0.0 688.7 jit_solution(17631098706521870149)
XLA Ops:
  17.1 230.6 %while.18 = (s32[]{:T(128)}, bf16[64,2,256]{2,0,1:T(8,128)(2,1)S(1)}, s32[64]{0:T(128)S(1)}, f32[4,8,64]{2,1,0:T(8,128)S(1)}, f32[4,8,64]{2,1,0:T(8,128)S(1)}, /...) while((s32[]{:T(128)}, ...), condition=%wide.region_5.6_spmd, body=%wide.region_2.5_spmd.sunk | while | flops 118759424 | bytes 3754157 | solution.py:80
  17.1 4.4 collective-permute-start.1
  21.5 3.5 collective-permute-start
  36.8 4.8 collective-permute-done.1
  41.6 4.9 collective-permute-done
  53.0 4.8 collective-permute-done.1
  67.7 4.4 collective-permute-done.1
  81.1 6.7 collective-permute-done.1
  87.9 21.1 %collective-permute-done = bf16[64,2,256]{2,0,1:T(8,128)(2,1)S(1)} collective-permute-done((bf16[64,2,256]{2,0,1:T(8,128)(2,1)S(1)}, bf16[64,2,256]{2,0,1:T(8,128)(2,1)S(1)}, u32[]{:S(2)}, u32[]{:S(2)}) %collective-permute-start) | collective-permute-done | bytes 65568 | tf_op jit(solution)/shard_map/while/body/eval_jaxpr/ppermute | solution.py:21
  115.4 4.8 collective-permute-done.1
  120.2 4.0 collective-permute-done
  130.7 4.4 collective-permute-done.1
  144.1 4.4 collective-permute-done.1
  157.5 4.4 collective-permute-done.1
  170.8 4.4 collective-permute-done.1
  184.2 4.7 collective-permute-done.1
  197.6 4.4 collective-permute-done.1
  211.0 4.4 collective-permute-done.1
  224.8 4.4 collective-permute-done.1
  238.2 4.4 collective-permute-done.1
  252.9 4.1 multiply_reduce_fusion.1
  260.2 16.6 %all_to_all.20 = bf16[8,16,2,1440]{3,2,0,1:T(2,128)(2,1)S(1)} all-to-all(bf16[8,16,2,1440]{3,2,0,1:T(2,128)(2,1)S(1)} %copy.69), channel_id=1, replica_groups=mesh['ctx'=16,'exp'=32] {'ctx'}, dimensions={1} | all-to-all | bytes 1474560 | tf_op jit(solution)/shard_map/all_to_all | solution.py:112
  280.1 183.4 %all_to_all.21 = bf16[32,16,2,1440]{3,2,1,0:T(2,128)(2,1)} all-to-all(bf16[32,16,2,1440]{3,2,1,0:T(2,128)(2,1)S(1)} %bitcast.67), channel_id=1, replica_groups=mesh['ctx'=16,'exp'=32] {'exp'}, dimensions={0} | all-to-all | bytes 5898240 | tf_op jit(solution)/shard_map/all_to_all | solution.py:114
  463.6 7.6 %reshape.250 = bf16[1024,1440]{1,0:T(8,128)(2,1)} reshape(bf16[32,16,2,1440]{3,2,1,0:T(2,128)(2,1)} %all_to_all.21) | data formatting | bytes 5898240 | tf_op jit(solution)/shard_map/reshape | solution.py:115
  471.2 4.4 fusion.37
  475.6 7.3 %convolution_convert_fusion = bf16[1024,1440]{0,1:T(8,128)(2,1)} fusion(bf16[360,1440]{1,0:T(8,128)(2,1)S(1)} %copy-done, f32[1024,360]{0,1:T(8,128)} %fusion.37, bf16[1024,1440]{1,0:T(8,128)(2,1)} %reshape.250, bf16[1440,360]{1,0:T(8,128)(2,1)} %param.24), kind=kOutput, calls=%fused_computation.19 | convolution fusion | flops 2127790080 | bytes 9446400 | tf_op jit(solution)/shard_map/dot_general | solution.py:120
  482.9 4.6 copy.71
  487.5 7.3 %reshape.251 = bf16[32,16,2,1440]{3,2,1,0:T(2,128)(2,1)} reshape(bf16[1024,1440]{1,0:T(8,128)(2,1)} %copy.71) | data formatting | bytes 5898240 | tf_op jit(solution)/shard_map/reshape | solution.py:122
  494.9 149.7 %all_to_all.22 = bf16[32,16,2,1440]{3,2,1,0:T(2,128)(2,1)S(1)} all-to-all(bf16[32,16,2,1440]{3,2,1,0:T(2,128)(2,1)} %reshape.251), channel_id=1, replica_groups=mesh['ctx'=16,'exp'=32] {'exp'}, dimensions={0} | all-to-all | bytes 5898240 | tf_op jit(solution)/shard_map/all_to_all | solution.py:119
  644.5 3.5 bitcast_reduce_fusion
  649.7 3.9 all-to-all-start.3
  653.7 21.3 %all-to-all-done.3 = bf16[8,16,2,1440]{3,2,0,1:T(2,128)(2,1)S(1)} async-done(((bf16[8,16,2,1440]{3,2,0,1:T(2,128)(2,1)}), bf16[8,16,2,1440]{3,2,0,1:T(2,128)(2,1)S(1)}, u32[]{:S(2)}, u32[]{:S(2)}) %all-to-all-start.3) | async-done | bytes 737312 | tf_op jit(solution)/shard_map/all_to_all | solution.py:131
  (295 shorter events, 156.7 us)
Async XLA Ops:
  6.5 246.3 %all-gather.2.cloned.1.call-start = ((), (), s32[]{:S(2)}) async-start(), calls=%async_computation.4 | async-start | bytes 6488064 | tf_op jit(solution)/shard_map/all_gather | solution.py:86
  17.1 10.5 %collective-permute-start.1 = (s32[64]{0:T(128)S(1)}, s32[64]{0:T(128)S(1)}, u32[]{:S(2)}, u32[]{:S(2)}) collective-permute-start(s32[64]{0:T(128)S(1)} %get-tuple-element.176), channel_id=1, source_target_pairs={{0,32},{32,64},{64,96},{96,128},{128,160},{160,192},{192,224},{224... | collective-permute-start | bytes 776 | tf_op jit(solution)/shard_map/while/body/eval_jaxpr/ppermute | solution.py:21
  21.5 8.9 %collective-permute-start = (bf16[64,2,256]{2,0,1:T(8,128)(2,1)S(1)}, bf16[64,2,256]{2,0,1:T(8,128)(2,1)S(1)}, u32[]{:S(2)}, u32[]{:S(2)}) collective-permute-start(bf16[64,2,256]{2,0,1:T(8,128)(2,1)S(1)} %get-tuple-element.175), channel_id=1, source_target_pairs={{0,32},{32,64},{64,96},{96,128},{128,160},{160,192},{192,224},{224... | collective-permute-start | bytes 196616 | tf_op jit(solution)/shard_map/while/body/eval_jaxpr/ppermute | solution.py:21
  32.9 8.6 %collective-permute-start.1 = (s32[64]{0:T(128)S(1)}, s32[64]{0:T(128)S(1)}, u32[]{:S(2)}, u32[]{:S(2)}) collective-permute-start(s32[64]{0:T(128)S(1)} %get-tuple-element.176), channel_id=1, source_target_pairs={{0,32},{32,64},{64,96},{96,128},{128,160},{160,192},{192,224},{224... | collective-permute-start | bytes 776 | tf_op jit(solution)/shard_map/while/body/eval_jaxpr/ppermute | solution.py:21
  34.8 11.7 %collective-permute-start = (bf16[64,2,256]{2,0,1:T(8,128)(2,1)S(1)}, bf16[64,2,256]{2,0,1:T(8,128)(2,1)S(1)}, u32[]{:S(2)}, u32[]{:S(2)}) collective-permute-start(bf16[64,2,256]{2,0,1:T(8,128)(2,1)S(1)} %get-tuple-element.175), channel_id=1, source_target_pairs={{0,32},{32,64},{64,96},{96,128},{128,160},{160,192},{192,224},{224... | collective-permute-start | bytes 196616 | tf_op jit(solution)/shard_map/while/body/eval_jaxpr/ppermute | solution.py:21
  49.1 8.6 %collective-permute-start.1 = (s32[64]{0:T(128)S(1)}, s32[64]{0:T(128)S(1)}, u32[]{:S(2)}, u32[]{:S(2)}) collective-permute-start(s32[64]{0:T(128)S(1)} %get-tuple-element.176), channel_id=1, source_target_pairs={{0,32},{32,64},{64,96},{96,128},{128,160},{160,192},{192,224},{224... | collective-permute-start | bytes 776 | tf_op jit(solution)/shard_map/while/body/eval_jaxpr/ppermute | solution.py:21
  51.0 10.3 %collective-permute-start = (bf16[64,2,256]{2,0,1:T(8,128)(2,1)S(1)}, bf16[64,2,256]{2,0,1:T(8,128)(2,1)S(1)}, u32[]{:S(2)}, u32[]{:S(2)}) collective-permute-start(bf16[64,2,256]{2,0,1:T(8,128)(2,1)S(1)} %get-tuple-element.175), channel_id=1, source_target_pairs={{0,32},{32,64},{64,96},{96,128},{128,160},{160,192},{192,224},{224... | collective-permute-start | bytes 196616 | tf_op jit(solution)/shard_map/while/body/eval_jaxpr/ppermute | solution.py:21
  63.8 8.2 %collective-permute-start.1 = (s32[64]{0:T(128)S(1)}, s32[64]{0:T(128)S(1)}, u32[]{:S(2)}, u32[]{:S(2)}) collective-permute-start(s32[64]{0:T(128)S(1)} %get-tuple-element.176), channel_id=1, source_target_pairs={{0,32},{32,64},{64,96},{96,128},{128,160},{160,192},{192,224},{224... | collective-permute-start | bytes 776 | tf_op jit(solution)/shard_map/while/body/eval_jaxpr/ppermute | solution.py:21
  65.8 8.9 %collective-permute-start = (bf16[64,2,256]{2,0,1:T(8,128)(2,1)S(1)}, bf16[64,2,256]{2,0,1:T(8,128)(2,1)S(1)}, u32[]{:S(2)}, u32[]{:S(2)}) collective-permute-start(bf16[64,2,256]{2,0,1:T(8,128)(2,1)S(1)} %get-tuple-element.175), channel_id=1, source_target_pairs={{0,32},{32,64},{64,96},{96,128},{128,160},{160,192},{192,224},{224... | collective-permute-start | bytes 196616 | tf_op jit(solution)/shard_map/while/body/eval_jaxpr/ppermute | solution.py:21
  77.2 10.6 %collective-permute-start.1 = (s32[64]{0:T(128)S(1)}, s32[64]{0:T(128)S(1)}, u32[]{:S(2)}, u32[]{:S(2)}) collective-permute-start(s32[64]{0:T(128)S(1)} %get-tuple-element.176), channel_id=1, source_target_pairs={{0,32},{32,64},{64,96},{96,128},{128,160},{160,192},{192,224},{224... | collective-permute-start | bytes 776 | tf_op jit(solution)/shard_map/while/body/eval_jaxpr/ppermute | solution.py:21
  79.2 29.8 %collective-permute-start = (bf16[64,2,256]{2,0,1:T(8,128)(2,1)S(1)}, bf16[64,2,256]{2,0,1:T(8,128)(2,1)S(1)}, u32[]{:S(2)}, u32[]{:S(2)}) collective-permute-start(bf16[64,2,256]{2,0,1:T(8,128)(2,1)S(1)} %get-tuple-element.175), channel_id=1, source_target_pairs={{0,32},{32,64},{64,96},{96,128},{128,160},{160,192},{192,224},{224... | collective-permute-start | bytes 196616 | tf_op jit(solution)/shard_map/while/body/eval_jaxpr/ppermute | solution.py:21
  111.5 8.6 %collective-permute-start.1 = (s32[64]{0:T(128)S(1)}, s32[64]{0:T(128)S(1)}, u32[]{:S(2)}, u32[]{:S(2)}) collective-permute-start(s32[64]{0:T(128)S(1)} %get-tuple-element.176), channel_id=1, source_target_pairs={{0,32},{32,64},{64,96},{96,128},{128,160},{160,192},{192,224},{224... | collective-permute-start | bytes 776 | tf_op jit(solution)/shard_map/while/body/eval_jaxpr/ppermute | solution.py:21
  113.5 10.8 %collective-permute-start = (bf16[64,2,256]{2,0,1:T(8,128)(2,1)S(1)}, bf16[64,2,256]{2,0,1:T(8,128)(2,1)S(1)}, u32[]{:S(2)}, u32[]{:S(2)}) collective-permute-start(bf16[64,2,256]{2,0,1:T(8,128)(2,1)S(1)} %get-tuple-element.175), channel_id=1, source_target_pairs={{0,32},{32,64},{64,96},{96,128},{128,160},{160,192},{192,224},{224... | collective-permute-start | bytes 196616 | tf_op jit(solution)/shard_map/while/body/eval_jaxpr/ppermute | solution.py:21
  126.8 8.2 %collective-permute-start.1 = (s32[64]{0:T(128)S(1)}, s32[64]{0:T(128)S(1)}, u32[]{:S(2)}, u32[]{:S(2)}) collective-permute-start(s32[64]{0:T(128)S(1)} %get-tuple-element.176), channel_id=1, source_target_pairs={{0,32},{32,64},{64,96},{96,128},{128,160},{160,192},{192,224},{224... | collective-permute-start | bytes 776 | tf_op jit(solution)/shard_map/while/body/eval_jaxpr/ppermute | solution.py:21
  128.7 8.9 %collective-permute-start = (bf16[64,2,256]{2,0,1:T(8,128)(2,1)S(1)}, bf16[64,2,256]{2,0,1:T(8,128)(2,1)S(1)}, u32[]{:S(2)}, u32[]{:S(2)}) collective-permute-start(bf16[64,2,256]{2,0,1:T(8,128)(2,1)S(1)} %get-tuple-element.175), channel_id=1, source_target_pairs={{0,32},{32,64},{64,96},{96,128},{128,160},{160,192},{192,224},{224... | collective-permute-start | bytes 196616 | tf_op jit(solution)/shard_map/while/body/eval_jaxpr/ppermute | solution.py:21
  140.2 8.2 %collective-permute-start.1 = (s32[64]{0:T(128)S(1)}, s32[64]{0:T(128)S(1)}, u32[]{:S(2)}, u32[]{:S(2)}) collective-permute-start(s32[64]{0:T(128)S(1)} %get-tuple-element.176), channel_id=1, source_target_pairs={{0,32},{32,64},{64,96},{96,128},{128,160},{160,192},{192,224},{224... | collective-permute-start | bytes 776 | tf_op jit(solution)/shard_map/while/body/eval_jaxpr/ppermute | solution.py:21
  142.1 8.9 %collective-permute-start = (bf16[64,2,256]{2,0,1:T(8,128)(2,1)S(1)}, bf16[64,2,256]{2,0,1:T(8,128)(2,1)S(1)}, u32[]{:S(2)}, u32[]{:S(2)}) collective-permute-start(bf16[64,2,256]{2,0,1:T(8,128)(2,1)S(1)} %get-tuple-element.175), channel_id=1, source_target_pairs={{0,32},{32,64},{64,96},{96,128},{128,160},{160,192},{192,224},{224... | collective-permute-start | bytes 196616 | tf_op jit(solution)/shard_map/while/body/eval_jaxpr/ppermute | solution.py:21
  153.6 8.2 %collective-permute-start.1 = (s32[64]{0:T(128)S(1)}, s32[64]{0:T(128)S(1)}, u32[]{:S(2)}, u32[]{:S(2)}) collective-permute-start(s32[64]{0:T(128)S(1)} %get-tuple-element.176), channel_id=1, source_target_pairs={{0,32},{32,64},{64,96},{96,128},{128,160},{160,192},{192,224},{224... | collective-permute-start | bytes 776 | tf_op jit(solution)/shard_map/while/body/eval_jaxpr/ppermute | solution.py:21
  155.5 8.9 %collective-permute-start = (bf16[64,2,256]{2,0,1:T(8,128)(2,1)S(1)}, bf16[64,2,256]{2,0,1:T(8,128)(2,1)S(1)}, u32[]{:S(2)}, u32[]{:S(2)}) collective-permute-start(bf16[64,2,256]{2,0,1:T(8,128)(2,1)S(1)} %get-tuple-element.175), channel_id=1, source_target_pairs={{0,32},{32,64},{64,96},{96,128},{128,160},{160,192},{192,224},{224... | collective-permute-start | bytes 196616 | tf_op jit(solution)/shard_map/while/body/eval_jaxpr/ppermute | solution.py:21
  167.0 8.2 %collective-permute-start.1 = (s32[64]{0:T(128)S(1)}, s32[64]{0:T(128)S(1)}, u32[]{:S(2)}, u32[]{:S(2)}) collective-permute-start(s32[64]{0:T(128)S(1)} %get-tuple-element.176), channel_id=1, source_target_pairs={{0,32},{32,64},{64,96},{96,128},{128,160},{160,192},{192,224},{224... | collective-permute-start | bytes 776 | tf_op jit(solution)/shard_map/while/body/eval_jaxpr/ppermute | solution.py:21
  168.9 8.9 %collective-permute-start = (bf16[64,2,256]{2,0,1:T(8,128)(2,1)S(1)}, bf16[64,2,256]{2,0,1:T(8,128)(2,1)S(1)}, u32[]{:S(2)}, u32[]{:S(2)}) collective-permute-start(bf16[64,2,256]{2,0,1:T(8,128)(2,1)S(1)} %get-tuple-element.175), channel_id=1, source_target_pairs={{0,32},{32,64},{64,96},{96,128},{128,160},{160,192},{192,224},{224... | collective-permute-start | bytes 196616 | tf_op jit(solution)/shard_map/while/body/eval_jaxpr/ppermute | solution.py:21
  180.4 8.5 %collective-permute-start.1 = (s32[64]{0:T(128)S(1)}, s32[64]{0:T(128)S(1)}, u32[]{:S(2)}, u32[]{:S(2)}) collective-permute-start(s32[64]{0:T(128)S(1)} %get-tuple-element.176), channel_id=1, source_target_pairs={{0,32},{32,64},{64,96},{96,128},{128,160},{160,192},{192,224},{224... | collective-permute-start | bytes 776 | tf_op jit(solution)/shard_map/while/body/eval_jaxpr/ppermute | solution.py:21
  182.3 8.9 %collective-permute-start = (bf16[64,2,256]{2,0,1:T(8,128)(2,1)S(1)}, bf16[64,2,256]{2,0,1:T(8,128)(2,1)S(1)}, u32[]{:S(2)}, u32[]{:S(2)}) collective-permute-start(bf16[64,2,256]{2,0,1:T(8,128)(2,1)S(1)} %get-tuple-element.175), channel_id=1, source_target_pairs={{0,32},{32,64},{64,96},{96,128},{128,160},{160,192},{192,224},{224... | collective-permute-start | bytes 196616 | tf_op jit(solution)/shard_map/while/body/eval_jaxpr/ppermute | solution.py:21
  193.8 8.2 %collective-permute-start.1 = (s32[64]{0:T(128)S(1)}, s32[64]{0:T(128)S(1)}, u32[]{:S(2)}, u32[]{:S(2)}) collective-permute-start(s32[64]{0:T(128)S(1)} %get-tuple-element.176), channel_id=1, source_target_pairs={{0,32},{32,64},{64,96},{96,128},{128,160},{160,192},{192,224},{224... | collective-permute-start | bytes 776 | tf_op jit(solution)/shard_map/while/body/eval_jaxpr/ppermute | solution.py:21
  195.7 8.9 %collective-permute-start = (bf16[64,2,256]{2,0,1:T(8,128)(2,1)S(1)}, bf16[64,2,256]{2,0,1:T(8,128)(2,1)S(1)}, u32[]{:S(2)}, u32[]{:S(2)}) collective-permute-start(bf16[64,2,256]{2,0,1:T(8,128)(2,1)S(1)} %get-tuple-element.175), channel_id=1, source_target_pairs={{0,32},{32,64},{64,96},{96,128},{128,160},{160,192},{192,224},{224... | collective-permute-start | bytes 196616 | tf_op jit(solution)/shard_map/while/body/eval_jaxpr/ppermute | solution.py:21
  207.2 8.2 %collective-permute-start.1 = (s32[64]{0:T(128)S(1)}, s32[64]{0:T(128)S(1)}, u32[]{:S(2)}, u32[]{:S(2)}) collective-permute-start(s32[64]{0:T(128)S(1)} %get-tuple-element.176), channel_id=1, source_target_pairs={{0,32},{32,64},{64,96},{96,128},{128,160},{160,192},{192,224},{224... | collective-permute-start | bytes 776 | tf_op jit(solution)/shard_map/while/body/eval_jaxpr/ppermute | solution.py:21
  209.1 9.3 %collective-permute-start = (bf16[64,2,256]{2,0,1:T(8,128)(2,1)S(1)}, bf16[64,2,256]{2,0,1:T(8,128)(2,1)S(1)}, u32[]{:S(2)}, u32[]{:S(2)}) collective-permute-start(bf16[64,2,256]{2,0,1:T(8,128)(2,1)S(1)} %get-tuple-element.175), channel_id=1, source_target_pairs={{0,32},{32,64},{64,96},{96,128},{128,160},{160,192},{192,224},{224... | collective-permute-start | bytes 196616 | tf_op jit(solution)/shard_map/while/body/eval_jaxpr/ppermute | solution.py:21
  220.9 8.2 %collective-permute-start.1 = (s32[64]{0:T(128)S(1)}, s32[64]{0:T(128)S(1)}, u32[]{:S(2)}, u32[]{:S(2)}) collective-permute-start(s32[64]{0:T(128)S(1)} %get-tuple-element.176), channel_id=1, source_target_pairs={{0,32},{32,64},{64,96},{96,128},{128,160},{160,192},{192,224},{224... | collective-permute-start | bytes 776 | tf_op jit(solution)/shard_map/while/body/eval_jaxpr/ppermute | solution.py:21
  222.9 8.9 %collective-permute-start = (bf16[64,2,256]{2,0,1:T(8,128)(2,1)S(1)}, bf16[64,2,256]{2,0,1:T(8,128)(2,1)S(1)}, u32[]{:S(2)}, u32[]{:S(2)}) collective-permute-start(bf16[64,2,256]{2,0,1:T(8,128)(2,1)S(1)} %get-tuple-element.175), channel_id=1, source_target_pairs={{0,32},{32,64},{64,96},{96,128},{128,160},{160,192},{192,224},{224... | collective-permute-start | bytes 196616 | tf_op jit(solution)/shard_map/while/body/eval_jaxpr/ppermute | solution.py:21
  234.3 8.2 %collective-permute-start.1 = (s32[64]{0:T(128)S(1)}, s32[64]{0:T(128)S(1)}, u32[]{:S(2)}, u32[]{:S(2)}) collective-permute-start(s32[64]{0:T(128)S(1)} %get-tuple-element.176), channel_id=1, source_target_pairs={{0,32},{32,64},{64,96},{96,128},{128,160},{160,192},{192,224},{224... | collective-permute-start | bytes 776 | tf_op jit(solution)/shard_map/while/body/eval_jaxpr/ppermute | solution.py:21
  236.3 8.9 %collective-permute-start = (bf16[64,2,256]{2,0,1:T(8,128)(2,1)S(1)}, bf16[64,2,256]{2,0,1:T(8,128)(2,1)S(1)}, u32[]{:S(2)}, u32[]{:S(2)}) collective-permute-start(bf16[64,2,256]{2,0,1:T(8,128)(2,1)S(1)} %get-tuple-element.175), channel_id=1, source_target_pairs={{0,32},{32,64},{64,96},{96,128},{128,160},{160,192},{192,224},{224... | collective-permute-start | bytes 196616 | tf_op jit(solution)/shard_map/while/body/eval_jaxpr/ppermute | solution.py:21
  649.7 25.3 %all-to-all-start.3 = ((bf16[8,16,2,1440]{3,2,0,1:T(2,128)(2,1)}), bf16[8,16,2,1440]{3,2,0,1:T(2,128)(2,1)S(1)}, u32[]{:S(2)}, u32[]{:S(2)}) async-start(bf16[8,16,2,1440]{3,2,0,1:T(2,128)(2,1)} %copy.72), calls=%async_computation.3 | async-start | bytes 1572864 | tf_op jit(solution)/shard_map/all_to_all | solution.py:131
  (8 other events, 500.7 us)
Sparse Core Ops, SparseCore 0:
  10.5 115.4 all-gather.1
where the time goes:
time: 690 us; the launch traced here: 689 us
  blocking collectives  350 us (51%)
  waiting for transfers between devices  151 us (22%)
  starting transfers between devices  65.6 us (10%)
  matrix products  48.6 us (7%)
  local copies, waits for them, and re-layouts  44.8 us (6%)
  between operations  13.7 us (2%)
  other arithmetic  13.4 us (2%)
    all_to_all x1, blocking collectives, body(): lax.all_to_all(copies, 'exp', split_axis=0, concat_axis=0, tiled=True)  183 us
    all_to_all x1, blocking collectives, body(): lax.all_to_all(jnp.dot(active, w_down, preferred_element_type=jnp.float32...  150 us
    ppermute x30, waiting for transfers between devices, passed_along(): lax.ppermute(value, axis, [(i, (i + by) % length) for i in range(length)])  129 us
    ppermute x30, starting transfers between devices, passed_along(): lax.ppermute(value, axis, [(i, (i + by) % length) for i in range(length)])  61.7 us
    dot_general x16, matrix products, attend_block(): jnp.einsum('gjrs,sgd->gjrd', weights, values.astype(jnp.float32), precisi...  22.6 us
    all_to_all x1, waiting for transfers between devices, body(): lax.all_to_all(result, 'ctx', split_axis=1, concat_axis=1, tiled=True)  21.3 us
    all_to_all x1, blocking collectives, body(): lax.all_to_all(outgoing, 'ctx', split_axis=1, concat_axis=1, tiled=True)  16.6 us
  transfers between devices with their start and end apart: 32, of which 31 were waited for; matrix products, arithmetic and copies ran while one was open for 8% of the time, Pallas kernels for 0%

commit v1 on v0

v1 whole, which is shorter than its diff:
```python
import functools
import math

import jax
import jax.numpy as jnp
from jax import lax
from jax.experimental import pallas as pl
from jax.experimental.pallas import tpu as pltpu
from jax.sharding import PartitionSpec as P

D = 1440
QH = 32
KVH = 4
HD = 64
TOP = 4
SLICES = 4
RUN = 32
EXPERTS = 128
LOG2E = math.log2(math.e)
NEG = -1e30
F32 = jnp.float32
BF16 = jnp.bfloat16


def attend_kernel(qpos_ref, sinks_ref, q_ref, kv_ref, out_ref, q_sc, k_sc, v_sc, bias_sc):
    rows = q_ref.shape[0]
    shards = kv_ref.shape[0]
    length = shards * rows
    group = QH // KVH
    for head in range(QH):
        q_sc[head // 2, (head % 2) * rows : (head % 2 + 1) * rows, :] = q_ref[
            :, head * HD : (head + 1) * HD
        ]
    kv = kv_ref[:, 0:rows, :].reshape(length, 2 * KVH * HD)
    ones = jnp.ones((length, HD), BF16)
    for g in range(KVH):
        k_sc[g] = kv[:, g * HD : (g + 1) * HD]
        v_sc[g] = jnp.concatenate(
            [kv[:, (KVH + g) * HD : (KVH + g + 1) * HD], ones], axis=1
        )
    number = jnp.concatenate([kv_ref[s, rows : rows + 1, 0:rows] for s in range(shards)], axis=1)
    lane = lax.broadcasted_iota(jnp.int32, (1, length), 1)
    key_pos = number.astype(F32).astype(jnp.int32) * RUN + lane % RUN
    bias = jnp.where(key_pos <= qpos_ref[...], 0.0, NEG).astype(F32)
    bias_sc[0:rows] = bias
    bias_sc[rows : 2 * rows] = bias
    pairs = group // 2

    def step(i, carry):
        g = i // pairs
        scores = lax.dot_general(
            q_sc[i], k_sc[g], (((1,), (1,)), ((), ())), preferred_element_type=F32
        )
        scores = scores * (LOG2E / math.sqrt(HD)) + bias_sc[...]
        row = lax.broadcasted_iota(jnp.int32, (2 * rows, 1), 0)
        sink = jnp.where(row < rows, sinks_ref[2 * i], sinks_ref[2 * i + 1]) * LOG2E
        top = jnp.maximum(jnp.max(scores, axis=1, keepdims=True), sink)
        weights = jnp.exp2(scores - top).astype(BF16)
        mixed = jnp.dot(weights, v_sc[g], preferred_element_type=F32)
        total = mixed[:, HD : HD + 1] + jnp.exp2(sink - top)
        result = (mixed[:, 0:HD] / total).astype(BF16)
        out_ref[:, pl.ds(pl.multiple_of(i * 2 * HD, 2 * HD), 2 * HD)] = jnp.concatenate(
            [result[0:rows], result[rows : 2 * rows]], axis=1
        )
        return carry

    lax.fori_loop(0, QH // 2, step, 0)


def attend(query, gathered, query_pos, sinks):
    rows = query.shape[0]
    shards = gathered.shape[0]
    length = shards * rows
    vmem = pl.BlockSpec(memory_space=pltpu.VMEM)
    return pl.pallas_call(
        attend_kernel,
        out_shape=jax.ShapeDtypeStruct((rows, QH * HD), BF16),
        in_specs=[vmem, pl.BlockSpec(memory_space=pltpu.SMEM), vmem, vmem],
        out_specs=vmem,
        scratch_shapes=[
            pltpu.VMEM((QH // 2, 2 * rows, HD), BF16),
            pltpu.VMEM((KVH, length, HD), BF16),
            pltpu.VMEM((KVH, length, 2 * HD), BF16),
            pltpu.VMEM((2 * rows, length), F32),
        ],
        compiler_params=pltpu.CompilerParams(vmem_limit_bytes=24 << 20),
        name="attend",
    )(query_pos[:, None], sinks, query, gathered)


def named(ids_ref, rank_cols):
    rows = ids_ref.shape[0]
    expert = lax.broadcasted_iota(jnp.int32, (rows, EXPERTS), 1)
    hits = [ids_ref[:, k : k + 1] == expert for k in range(TOP)]
    any_hit = functools.reduce(jnp.logical_or, hits)
    mask = any_hit.astype(F32)
    before = (
        lax.broadcasted_iota(jnp.int32, (rows, rows), 1)
        < lax.broadcasted_iota(jnp.int32, (rows, rows), 0)
    ).astype(F32)
    earlier = jnp.dot(
        before.astype(BF16), mask.astype(BF16), preferred_element_type=F32
    )
    first = mask * (earlier < 0.5).astype(F32)
    second = mask - first
    return hits, first, second


def project_kernel(att_ref, ow_ref, resid_ref, gain_ref, ids_ref, mixed_ref, out_ref, acc):
    @pl.when(pl.program_id(0) == 0)
    def _():
        acc[...] = resid_ref[...].astype(F32)

    acc[...] += jnp.dot(att_ref[...], ow_ref[...], preferred_element_type=F32)

    @pl.when(pl.program_id(0) == pl.num_programs(0) - 1)
    def _():
        mixed = acc[...]
        mixed_ref[...] = mixed
        scale = lax.rsqrt(jnp.mean(mixed * mixed, axis=1, keepdims=True) + 1e-05)
        normed = (mixed * scale * gain_ref[...]).astype(BF16)
        _, first, second = named(ids_ref, None)
        chosen = jnp.concatenate([first, second], axis=1).astype(BF16)
        out_ref[...] = lax.dot_general(
            chosen, normed, (((0,), (0,)), ((), ())), preferred_element_type=F32
        ).astype(BF16)


def project(attended, o_weight, resid, gain, ids):
    rows = attended.shape[0]
    depth = o_weight.shape[0]
    tile = 512
    whole = lambda i: (0, 0)
    return pl.pallas_call(
        project_kernel,
        grid=(depth // tile,),
        out_shape=(
            jax.ShapeDtypeStruct((rows, D), F32),
            jax.ShapeDtypeStruct((rows * TOP, D), BF16),
        ),
        in_specs=[
            pl.BlockSpec((rows, tile), lambda i: (0, i)),
            pl.BlockSpec((tile, D), lambda i: (i, 0)),
            pl.BlockSpec((rows, D), whole),
            pl.BlockSpec((1, D), whole),
            pl.BlockSpec((rows, TOP), whole),
        ],
        out_specs=(pl.BlockSpec((rows, D), whole), pl.BlockSpec((rows * TOP, D), whole)),
        scratch_shapes=[pltpu.VMEM((rows, D), F32)],
        compiler_params=pltpu.CompilerParams(vmem_limit_bytes=24 << 20),
        name="project",
    )(attended, o_weight, resid, gain[None, :], ids)


def experts_kernel(x_ref, *refs):
    n = 3 * SLICES
    weights, out_ref = refs[:n], refs[n]
    held, sems = refs[n + 1 : 2 * n + 1], refs[2 * n + 1]
    copies = [
        pltpu.make_async_copy(weights[i], held[i], sems.at[i]) for i in range(n)
    ]
    for copy in copies:
        copy.start()
    x = x_ref[...]
    total = None
    for s in range(SLICES):
        copies[3 * s].wait()
        gate = jnp.dot(x, held[3 * s][...], preferred_element_type=F32)
        copies[3 * s + 1].wait()
        up = jnp.dot(x, held[3 * s + 1][...], preferred_element_type=F32)
        active = (gate * jax.nn.sigmoid(1.702 * gate) * (up + 1.0)).astype(BF16)
        copies[3 * s + 2].wait()
        part = jnp.dot(active, held[3 * s + 2][...], preferred_element_type=F32)
        total = part if total is None else total + part
    out_ref[...] = total.astype(BF16)


def experts(x, weights):
    vmem = pl.BlockSpec(memory_space=pltpu.VMEM)
    return pl.pallas_call(
        experts_kernel,
        out_shape=jax.ShapeDtypeStruct(x.shape, BF16),
        in_specs=[vmem] + [pl.BlockSpec(memory_space=pl.ANY)] * len(weights),
        out_specs=vmem,
        scratch_shapes=[pltpu.VMEM(w.shape, w.dtype) for w in weights]
        + [pltpu.SemaphoreType.DMA((len(weights),))],
        compiler_params=pltpu.CompilerParams(vmem_limit_bytes=28 << 20),
        name="experts",
    )(x, *weights)


def combine_kernel(ids_ref, rw_ref, mixed_ref, back_ref, out_ref):
    hits, first, second = named(ids_ref, None)
    share = sum(
        jnp.where(hits[k], rw_ref[:, k : k + 1], 0.0) for k in range(TOP)
    )
    both = jnp.concatenate([share * first, share * second], axis=1)
    high = both.astype(BF16)
    low = (both - high.astype(F32)).astype(BF16)
    back = back_ref[...]
    out_ref[...] = (
        mixed_ref[...]
        + jnp.dot(high, back, preferred_element_type=F32)
        + jnp.dot(low, back, preferred_element_type=F32)
    ).astype(BF16)


def combine(ids, shares, mixed, back):
    vmem = pl.BlockSpec(memory_space=pltpu.VMEM)
    return pl.pallas_call(
        combine_kernel,
        out_shape=jax.ShapeDtypeStruct(mixed.shape, BF16),
        in_specs=[vmem] * 4,
        out_specs=vmem,
        compiler_params=pltpu.CompilerParams(vmem_limit_bytes=16 << 20),
        name="combine",
    )(ids, shares, mixed, back)


def swapped(value, bit):
    n = lax.axis_size("exp")
    return lax.ppermute(value, "exp", [(i, i ^ bit) for i in range(n)])


def body(
    query,
    key_value,
    positions,
    resid,
    sinks,
    o_weight,
    norm_gain,
    expert_ids,
    route_weights,
    w_gate,
    w_up,
    w_down,
):
    n_ctx, n_exp = lax.axis_size("ctx"), lax.axis_size("exp")
    rows = query.shape[1]
    pos = positions[0]
    numbers = jnp.broadcast_to((pos // RUN).astype(BF16)[None, :], (8, rows))
    own = jnp.concatenate(
        [
            key_value[0].reshape(rows, 2 * KVH * HD),
            jnp.pad(numbers, ((0, 0), (0, 2 * KVH * HD - rows))),
        ],
        axis=0,
    )
    gathered = lax.all_to_all(
        jnp.broadcast_to(own[None], (n_ctx,) + own.shape), "ctx", 0, 0, tiled=True
    )
    mine = (w_gate, w_up, w_down)
    beside = tuple(swapped(w, 2) for w in mine)
    core = tuple(swapped(w, 1) for w in mine)
    core_beside = tuple(swapped(w, 1) for w in beside)
    all_o = lax.all_gather(o_weight, "exp", axis=0, tiled=True)

    attended = attend(query[0], gathered, pos, sinks)
    mixed, outgoing = project(attended, all_o, resid[0], norm_gain, expert_ids[0])

    per_row = n_exp // SLICES
    members = [
        [
            (e // per_row) * n_exp + (e % per_row) * SLICES + 2 * rank + side
            for rank in range(2)
            for e in range(EXPERTS)
        ]
        for side in range(2)
    ]

    def exchange(value):
        return lax.all_to_all(
            value.reshape(2 * EXPERTS, 1, D),
            ("ctx", "exp"),
            0,
            0,
            tiled=True,
            axis_index_groups=members,
        ).reshape(2 * EXPERTS, D)

    arrived = exchange(outgoing)
    done = experts(arrived, mine + core + beside + core_beside)
    back = exchange(done)
    return combine(expert_ids[0], route_weights[0], mixed, back)[None]


def solution(mesh):
    return jax.shard_map(
        body,
        mesh=mesh,
        in_specs=(
            P("exp", "ctx", None),
            P("exp", "ctx", None, None),
            P("exp", "ctx"),
            P("exp", "ctx", None),
            P(),
            P("exp", None),
            P(),
            P("exp", "ctx", None),
            P("exp", "ctx", None),
            P(None, ("ctx", "exp")),
            P(None, ("ctx", "exp")),
            P(("ctx", "exp"), None),
        ),
        out_specs=P("exp", "ctx", None),
        check_vma=False,
    )
```

time: 690 us -> 345 us (0.50)
  blocking collectives: 350 us -> 0 us
  waiting for transfers between devices: 151 us -> 209 us
  matrix products: 48.6 us -> 0 us
  local copies, waits for them, and re-layouts: 44.8 us -> 21.6 us
  Pallas kernels: 0 us -> 22.5 us
  other arithmetic: 13.4 us -> 3.19 us
    all_to_all x3 -> x0, blocking collectives: 350 us -> none  [the longest x1 183 us: body(): lax.all_to_all(copies, 'exp', split_axis=0, concat_axis=0, tiled=True)]
    ppermute x30 -> x9, waiting for transfers between devices: 129 us -> 60.9 us  [swapped(): return lax.ppermute(value, 'exp', [(i, i ^ bit) for i in range(n)])]
    all_gather x1, waiting for transfers between devices: 0.02 us -> 66.3 us  [body(): all_o = lax.all_gather(o_weight, 'exp', axis=0, tiled=True)]
    all_to_all x1 -> x3, waiting for transfers between devices: 21.3 us -> 80.6 us  [the longest x1 41.1 us: body(): lax.all_to_all(jnp.broadcast_to(own[None], (n_ctx,) + own.shape), 'ctx',...]
    dot_general x35 -> x0, matrix products: 48.6 us -> none  [the longest x16 22.6 us: attend_block(): jnp.einsum('gjrs,sgd->gjrd', weights, values.astype(jnp.float32), precisi...]
    all_to_all x1 -> x3, starting transfers between devices: 3.92 us -> 44.8 us  [the longest x2 35.5 us: exchange(): lax.all_to_all(value.reshape(2 * EXPERTS, 1, D), ('ctx', 'exp'), 0, 0, ti...]
    ppermute x30 -> x9, starting transfers between devices: 61.7 us -> 26.3 us  [swapped(): return lax.ppermute(value, 'exp', [(i, i ^ bit) for i in range(n)])]
    pallas_call x0 -> x4, Pallas kernels: none -> 22.5 us  [the longest x1 11.5 us: attend(): pl.pallas_call(attend_kernel, out_shape=jax.ShapeDtypeStruct((rows, QH *...]
  transfers between devices with their start and end apart: 32 -> 13, of which waited for: 31 -> 6; matrix products, arithmetic and copies ran while one was open for 8% -> 3% of each run, Pallas kernels for 0% -> 3%
where the time goes in v1:
time: 345 us; the launch traced here: 341 us
  waiting for transfers between devices  209 us (61%)
  starting transfers between devices  71.1 us (21%)
  Pallas kernels  22.5 us (7%)
  local copies, waits for them, and re-layouts  21.6 us (6%)
  between operations  13.7 us (4%)
    all_gather x1, waiting for transfers between devices, body(): all_o = lax.all_gather(o_weight, 'exp', axis=0, tiled=True)  66.3 us
    ppermute x9, waiting for transfers between devices, swapped(): return lax.ppermute(value, 'exp', [(i, i ^ bit) for i in range(n)])  60.9 us
    all_to_all x1, waiting for transfers between devices, body(): lax.all_to_all(jnp.broadcast_to(own[None], (n_ctx,) + own.shape), 'ctx',...  41.1 us
    all_to_all x2, waiting for transfers between devices, exchange(): lax.all_to_all(value.reshape(2 * EXPERTS, 1, D), ('ctx', 'exp'), 0, 0, ti...  39.6 us
    all_to_all x2, starting transfers between devices, exchange(): lax.all_to_all(value.reshape(2 * EXPERTS, 1, D), ('ctx', 'exp'), 0, 0, ti...  35.5 us
    ppermute x9, starting transfers between devices, swapped(): return lax.ppermute(value, 'exp', [(i, i ^ bit) for i in range(n)])  26.3 us
    unnamed x39, local copies, waits for them, and re-layouts  18.1 us
    pallas_call x1, Pallas kernels, attend(): pl.pallas_call(attend_kernel, out_shape=jax.ShapeDtypeStruct((rows, QH *...  11.5 us
  transfers between devices with their start and end apart: 13, of which 6 were waited for; matrix products, arithmetic and copies ran while one was open for 3% of the time, Pallas kernels for 3%

profile of v1, /device:TPU:1, one launch (start us, length us, event | category | flops | bytes accessed | tf_op | source)
XLA Modules:
  0.0 340.7 jit_solution(3287257110153536996)
XLA Ops:
  8.8 1.1 broadcast_in_dim.9
  9.9 9.3 %all-to-all-start = ((bf16[16,72,512]{2,1,0:T(8,128)(2,1)}), bf16[16,72,512]{2,1,0:T(8,128)(2,1)S(1)}, u32[]{:S(2)}, u32[]{:S(2)}) async-start(bf16[16,72,512]{2,1,0:T(8,128)(2,1)} %broadcast_in_dim.9), calls=%async_computation | async-start | bytes 2359296 | tf_op jit(solution)/shard_map/all_to_all | solution.py:250
  19.5 41.1 %all-to-all-done.kv_ref = bf16[16,72,512]{2,1,0:T(8,128)(2,1)S(1)} async-done(((bf16[16,72,512]{2,1,0:T(8,128)(2,1)}), bf16[16,72,512]{2,1,0:T(8,128)(2,1)S(1)}, u32[]{:S(2)}, u32[]{:S(2)}) %all-to-all-start) | async-done | bytes 1179680 | tf_op jit(solution)/shard_map/all_to_all | solution.py:250
  60.5 11.5 %attend.1.att_ref = bf16[64,2048]{1,0:T(8,128)(2,1)S(1)} custom-call(s32[64,1]{1,0:T(8,128)S(1)} %copy.23.qpos_ref, f32[32]{0:T(128)S(1)} %copy-done.11, bf16[64,2048]{1,0:T(8,128)(2,1)S(1)} %bitcast.27, bf16[16,72,512]{2,1,0:T(8,128)(2,1)S(1)} %all-to-all-done.kv_ref), custom_call_target="tpu_custom_call" | custom-call | tf_op jit(solution)/shard_map/attend/pallas_call | solution.py:75
  72.0 66.3 %all-gather.2.cloned.1.call-done.ow_ref = bf16[2048,1440]{1,0:T(8,128)(2,1)} async-done(((bf16[64,1440]{1,0:T(8,128)(2,1)}), bf16[2048,1440]{1,0:T(8,128)(2,1)}) %all-gather.2.cloned.1.call-update) | async-done | bytes 5898256 | tf_op jit(solution)/shard_map/all_gather | solution.py:257
  138.3 2.8 copy-done
  141.1 2.3 project.1
  144.6 1.3 reduce
  146.0 1.7 reshape.17
  147.7 16.0 %all-to-all-start.1 = ((bf16[256,2,720]{2,1,0:T(2,128)(2,1)}), bf16[256,2,720]{2,1,0:T(2,128)(2,1)}, u32[]{:S(2)}, u32[]{:S(2)}) async-start(bf16[256,2,720]{2,1,0:T(2,128)(2,1)} %reshape.17), calls=%async_computation.1 | async-start | bytes 1572864 | tf_op jit(solution)/shard_map/all_to_all | solution.py:273
  163.7 2.3 collective-permute-start.3
  166.0 3.0 collective-permute-start.4
  169.0 2.3 collective-permute-start.5
  171.3 3.6 %collective-permute-start = (bf16[1440,360]{1,0:T(8,128)(2,1)S(1)}, bf16[1440,360]{1,0:T(8,128)(2,1)S(1)}, u32[]{:S(2)}, u32[]{:S(2)}) collective-permute-start(bf16[1440,360]{1,0:T(8,128)(2,1)S(1)} %copy-done.1), channel_id=1, source_target_pairs={{0,1},{1,0},{2,3},{3,2},{4,5},{5,4},{6,7},{7,6},{8,9},{9,8},{10,11... | collective-permute-start | bytes 3110408 | tf_op jit(solution)/shard_map/ppermute | solution.py:222
  174.9 1.9 collective-permute-start.1
  176.8 21.2 %collective-permute-done.3.refs_6_ = bf16[1440,360]{1,0:T(8,128)(2,1)} collective-permute-done((bf16[1440,360]{1,0:T(8,128)(2,1)S(1)}, bf16[1440,360]{1,0:T(8,128)(2,1)}, u32[]{:S(2)}, u32[]{:S(2)}) %collective-permute-start.3) | collective-permute-done | bytes 1036832 | tf_op jit(solution)/shard_map/ppermute | solution.py:222
  198.0 4.1 %collective-permute-start.2 = (bf16[360,1440]{1,0:T(8,128)(2,1)S(1)}, bf16[360,1440]{1,0:T(8,128)(2,1)}, u32[]{:S(2)}, u32[]{:S(2)}) collective-permute-start(bf16[360,1440]{1,0:T(8,128)(2,1)S(1)} %copy-done.3), channel_id=1, source_target_pairs={{0,1},{1,0},{2,3},{3,2},{4,5},{5,4},{6,7},{7,6},{8,9},{9,8},{10,11... | collective-permute-start | bytes 3110408 | tf_op jit(solution)/shard_map/ppermute | solution.py:222
  202.1 19.9 %collective-permute-done.4.refs_7_ = bf16[1440,360]{1,0:T(8,128)(2,1)} collective-permute-done((bf16[1440,360]{1,0:T(8,128)(2,1)S(1)}, bf16[1440,360]{1,0:T(8,128)(2,1)}, u32[]{:S(2)}, u32[]{:S(2)}) %collective-permute-start.4) | collective-permute-done | bytes 1036832 | tf_op jit(solution)/shard_map/ppermute | solution.py:222
  222.1 3.9 %collective-permute-start.6 = (bf16[1440,360]{1,0:T(8,128)(2,1)}, bf16[1440,360]{1,0:T(8,128)(2,1)}, u32[]{:S(2)}, u32[]{:S(2)}) collective-permute-start(bf16[1440,360]{1,0:T(8,128)(2,1)} %collective-permute-done.3.refs_6_), channel_id=1, source_target_pairs={{0,1},{1,0},{2,3},{3,2},{4,5},{5,4},{6,7},{7,6},{8,9},{9,8},{10,11... | collective-permute-start | bytes 3110408 | tf_op jit(solution)/shard_map/ppermute | solution.py:222
  226.0 19.8 %collective-permute-done.5.refs_8_ = bf16[360,1440]{1,0:T(8,128)(2,1)} collective-permute-done((bf16[360,1440]{1,0:T(8,128)(2,1)S(1)}, bf16[360,1440]{1,0:T(8,128)(2,1)}, u32[]{:S(2)}, u32[]{:S(2)}) %collective-permute-start.5) | collective-permute-done | bytes 1036832 | tf_op jit(solution)/shard_map/ppermute | solution.py:222
  245.8 3.1 collective-permute-start.7
  248.9 1.0 copy-done.5
  249.9 2.1 collective-permute-start.8
  252.0 6.5 %reshape.18 = bf16[256,1,1440]{2,1,0:T(2,128)(2,1)} reshape(bf16[256,2,720]{2,1,0:T(2,128)(2,1)} %all-to-all-done.1) | data formatting | bytes 1474560
  258.6 1.7 copy.36
  260.6 7.5 %experts.1 = bf16[256,1440]{1,0:T(8,128)(2,1)S(1)} custom-call(bf16[256,1440]{1,0:T(8,128)(2,1)S(1)} %bitcast.22, bf16[1440,360]{1,0:T(8,128)(2,1)S(1)} %copy-done.1, bf16[1440,360]{1,0:T(8,128)(2,1)S(1)} %copy-done.2, bf16[360,1440]{1,0:T(8,128)(2,1)S(1)} %copy-done.4, bf16[1440,360]{1,0:T(8,128)(2,1)S(1)} %copy-done.6, ...), custom_call_target="tpu_custom_call" | custom-call | tf_op jit(solution)/shard_map/experts/pallas_call | solution.py:180
  268.1 1.2 reduce.1
  269.4 1.7 reshape.19
  271.1 19.5 %all-to-all-start.2 = ((bf16[256,2,720]{2,1,0:T(2,128)(2,1)}), bf16[256,2,720]{2,1,0:T(2,128)(2,1)S(1)}, u32[]{:S(2)}, u32[]{:S(2)}) async-start(bf16[256,2,720]{2,1,0:T(2,128)(2,1)} %reshape.19), calls=%async_computation.2 | async-start | bytes 1572864 | tf_op jit(solution)/shard_map/all_to_all | solution.py:273
  290.7 39.6 %all-to-all-done.2 = bf16[256,2,720]{2,1,0:T(2,128)(2,1)S(1)} async-done(((bf16[256,2,720]{2,1,0:T(2,128)(2,1)}), bf16[256,2,720]{2,1,0:T(2,128)(2,1)S(1)}, u32[]{:S(2)}, u32[]{:S(2)}) %all-to-all-start.2) | async-done | bytes 737312 | tf_op jit(solution)/shard_map/all_to_all | solution.py:273
  330.3 1.4 reshape.20
  332.6 1.3 combine.1
  (50 shorter events, 5.2 us)
Async XLA Ops:
  6.5 131.7 %all-gather.2.cloned.1.call-start = ((), (), s32[]{:S(2)}) async-start(), calls=%async_computation.3 | async-start | bytes 6488064 | tf_op jit(solution)/shard_map/all_gather | solution.py:257
  9.9 9.4 %copy-start.13 = (s32[1,64,4]{1,2,0:T(4,128)S(1)}, s32[1,64,4]{1,2,0:T(4,128)}, u32[]{:S(2)}) copy-start(s32[1,64,4]{1,2,0:T(4,128)} %param.19) | copy-start | bytes 3076
  9.9 9.5 %copy-start.15 = (s32[1,64]{1,0:T(1,128)S(1)}, s32[1,64]{1,0:T(1,128)}, u32[]{:S(2)}) copy-start(s32[1,64]{1,0:T(1,128)} %param.14) | copy-start | bytes 772
  9.9 9.6 %copy-start.12 = (f32[1440]{0:T(1024)S(1)}, f32[1440]{0:T(1024)}, u32[]{:S(2)}) copy-start(f32[1440]{0:T(1024)} %param.18) | copy-start | bytes 17284
  9.9 50.7 %copy-start.9 = (bf16[1,64,2048]{2,1,0:T(8,128)(2,1)S(1)}, bf16[1,64,2048]{2,1,0:T(8,128)(2,1)}, u32[]{:S(2)}) copy-start(bf16[1,64,2048]{2,1,0:T(8,128)(2,1)} %param.12) | copy-start | bytes 786436
  9.9 50.7 %copy-start.11 = (f32[32]{0:T(128)S(1)}, f32[32]{0:T(128)}, u32[]{:S(2)}) copy-start(f32[32]{0:T(128)} %sinks_ref.1) | copy-start | bytes 388
  9.9 50.6 %all-to-all-start = ((bf16[16,72,512]{2,1,0:T(8,128)(2,1)}), bf16[16,72,512]{2,1,0:T(8,128)(2,1)S(1)}, u32[]{:S(2)}, u32[]{:S(2)}) async-start(bf16[16,72,512]{2,1,0:T(8,128)(2,1)} %broadcast_in_dim.9), calls=%async_computation | async-start | bytes 2359296 | tf_op jit(solution)/shard_map/all_to_all | solution.py:250
  19.2 119.0 %copy-start.10 = (bf16[1,64,1440]{2,1,0:T(8,128)(2,1)S(1)}, bf16[1,64,1440]{2,1,0:T(8,128)(2,1)}, u32[]{:S(2)}) copy-start(bf16[1,64,1440]{2,1,0:T(8,128)(2,1)} %param.15) | copy-start | bytes 552964
  138.3 2.8 copy-start
  143.4 0.8 copy-start.7
  144.6 24.3 %copy-start.3 = (bf16[360,1440]{1,0:T(8,128)(2,1)S(1)}, bf16[360,1440]{1,0:T(8,128)(2,1)}, u32[]{:S(2)}) copy-start(bf16[360,1440]{1,0:T(8,128)(2,1)} %refs_2_.1) | copy-start | bytes 3110404
  145.9 20.0 %copy-start.2 = (bf16[1440,360]{1,0:T(8,128)(2,1)S(1)}, bf16[1440,360]{1,0:T(8,128)(2,1)}, u32[]{:S(2)}) copy-start(bf16[1440,360]{1,0:T(8,128)(2,1)} %refs_1_.1) | copy-start | bytes 3110404
  147.7 16.0 %copy-start.1 = (bf16[1440,360]{1,0:T(8,128)(2,1)S(1)}, bf16[1440,360]{1,0:T(8,128)(2,1)}, u32[]{:S(2)}) copy-start(bf16[1440,360]{1,0:T(8,128)(2,1)} %refs_0_.1) | copy-start | bytes 3110404
  147.7 104.3 %all-to-all-start.1 = ((bf16[256,2,720]{2,1,0:T(2,128)(2,1)}), bf16[256,2,720]{2,1,0:T(2,128)(2,1)}, u32[]{:S(2)}, u32[]{:S(2)}) async-start(bf16[256,2,720]{2,1,0:T(2,128)(2,1)} %reshape.17), calls=%async_computation.1 | async-start | bytes 1572864 | tf_op jit(solution)/shard_map/all_to_all | solution.py:273
  163.7 34.3 %collective-permute-start.3 = (bf16[1440,360]{1,0:T(8,128)(2,1)S(1)}, bf16[1440,360]{1,0:T(8,128)(2,1)}, u32[]{:S(2)}, u32[]{:S(2)}) collective-permute-start(bf16[1440,360]{1,0:T(8,128)(2,1)S(1)} %copy-done.1), channel_id=1, source_target_pairs={{0,2},{1,3},{2,0},{3,1},{4,6},{5,7},{6,4},{7,5},{8,10},{9,11},{10,... | collective-permute-start | bytes 3110408 | tf_op jit(solution)/shard_map/ppermute | solution.py:222
  166.0 56.1 %collective-permute-start.4 = (bf16[1440,360]{1,0:T(8,128)(2,1)S(1)}, bf16[1440,360]{1,0:T(8,128)(2,1)}, u32[]{:S(2)}, u32[]{:S(2)}) collective-permute-start(bf16[1440,360]{1,0:T(8,128)(2,1)S(1)} %copy-done.2), channel_id=1, source_target_pairs={{0,2},{1,3},{2,0},{3,1},{4,6},{5,7},{6,4},{7,5},{8,10},{9,11},{10,... | collective-permute-start | bytes 3110408 | tf_op jit(solution)/shard_map/ppermute | solution.py:222
  169.0 76.8 %collective-permute-start.5 = (bf16[360,1440]{1,0:T(8,128)(2,1)S(1)}, bf16[360,1440]{1,0:T(8,128)(2,1)}, u32[]{:S(2)}, u32[]{:S(2)}) collective-permute-start(bf16[360,1440]{1,0:T(8,128)(2,1)S(1)} %copy-done.3), channel_id=1, source_target_pairs={{0,2},{1,3},{2,0},{3,1},{4,6},{5,7},{6,4},{7,5},{8,10},{9,11},{10,... | collective-permute-start | bytes 3110408 | tf_op jit(solution)/shard_map/ppermute | solution.py:222
  171.3 77.6 %collective-permute-start = (bf16[1440,360]{1,0:T(8,128)(2,1)S(1)}, bf16[1440,360]{1,0:T(8,128)(2,1)S(1)}, u32[]{:S(2)}, u32[]{:S(2)}) collective-permute-start(bf16[1440,360]{1,0:T(8,128)(2,1)S(1)} %copy-done.1), channel_id=1, source_target_pairs={{0,1},{1,0},{2,3},{3,2},{4,5},{5,4},{6,7},{7,6},{8,9},{9,8},{10,11... | collective-permute-start | bytes 3110408 | tf_op jit(solution)/shard_map/ppermute | solution.py:222
  174.9 85.3 %collective-permute-start.1 = (bf16[1440,360]{1,0:T(8,128)(2,1)S(1)}, bf16[1440,360]{1,0:T(8,128)(2,1)}, u32[]{:S(2)}, u32[]{:S(2)}) collective-permute-start(bf16[1440,360]{1,0:T(8,128)(2,1)S(1)} %copy-done.2), channel_id=1, source_target_pairs={{0,1},{1,0},{2,3},{3,2},{4,5},{5,4},{6,7},{7,6},{8,9},{9,8},{10,11... | collective-permute-start | bytes 3110408 | tf_op jit(solution)/shard_map/ppermute | solution.py:222
  198.0 62.3 %collective-permute-start.2 = (bf16[360,1440]{1,0:T(8,128)(2,1)S(1)}, bf16[360,1440]{1,0:T(8,128)(2,1)}, u32[]{:S(2)}, u32[]{:S(2)}) collective-permute-start(bf16[360,1440]{1,0:T(8,128)(2,1)S(1)} %copy-done.3), channel_id=1, source_target_pairs={{0,1},{1,0},{2,3},{3,2},{4,5},{5,4},{6,7},{7,6},{8,9},{9,8},{10,11... | collective-permute-start | bytes 3110408 | tf_op jit(solution)/shard_map/ppermute | solution.py:222
  222.1 38.2 %collective-permute-start.6 = (bf16[1440,360]{1,0:T(8,128)(2,1)}, bf16[1440,360]{1,0:T(8,128)(2,1)}, u32[]{:S(2)}, u32[]{:S(2)}) collective-permute-start(bf16[1440,360]{1,0:T(8,128)(2,1)} %collective-permute-done.3.refs_6_), channel_id=1, source_target_pairs={{0,1},{1,0},{2,3},{3,2},{4,5},{5,4},{6,7},{7,6},{8,9},{9,8},{10,11... | collective-permute-start | bytes 3110408 | tf_op jit(solution)/shard_map/ppermute | solution.py:222
  245.8 14.5 %collective-permute-start.7 = (bf16[1440,360]{1,0:T(8,128)(2,1)}, bf16[1440,360]{1,0:T(8,128)(2,1)}, u32[]{:S(2)}, u32[]{:S(2)}) collective-permute-start(bf16[1440,360]{1,0:T(8,128)(2,1)} %collective-permute-done.4.refs_7_), channel_id=1, source_target_pairs={{0,1},{1,0},{2,3},{3,2},{4,5},{5,4},{6,7},{7,6},{8,9},{9,8},{10,11... | collective-permute-start | bytes 3110408 | tf_op jit(solution)/shard_map/ppermute | solution.py:222
  248.9 1.0 copy-start.5
  249.9 10.4 %collective-permute-start.8 = (bf16[360,1440]{1,0:T(8,128)(2,1)}, bf16[360,1440]{1,0:T(8,128)(2,1)}, u32[]{:S(2)}, u32[]{:S(2)}) collective-permute-start(bf16[360,1440]{1,0:T(8,128)(2,1)} %collective-permute-done.5.refs_8_), channel_id=1, source_target_pairs={{0,1},{1,0},{2,3},{3,2},{4,5},{5,4},{6,7},{7,6},{8,9},{9,8},{10,11... | collective-permute-start | bytes 3110408 | tf_op jit(solution)/shard_map/ppermute | solution.py:222
  258.6 1.7 copy-start.4
  258.6 2.0 copy-start.6
  271.1 19.5 %copy-start.14 = (f32[1,64,4]{1,2,0:T(4,128)S(1)}, f32[1,64,4]{1,2,0:T(4,128)}, u32[]{:S(2)}) copy-start(f32[1,64,4]{1,2,0:T(4,128)} %param.20) | copy-start | bytes 3076
  271.1 59.2 %all-to-all-start.2 = ((bf16[256,2,720]{2,1,0:T(2,128)(2,1)}), bf16[256,2,720]{2,1,0:T(2,128)(2,1)S(1)}, u32[]{:S(2)}, u32[]{:S(2)}) async-start(bf16[256,2,720]{2,1,0:T(2,128)(2,1)} %reshape.19), calls=%async_computation.2 | async-start | bytes 1572864 | tf_op jit(solution)/shard_map/all_to_all | solution.py:273
  331.6 1.0 copy-start.8
Sparse Core Ops, SparseCore 0:
  10.5 127.7 all-gather.1
